TPU v7x, 32 devices: a whole 2x2x4 slice. The times are simulated.
32 devices in a mesh: dp: 8 (over y, x, core), tensor: 4 (over z).
Axes of the slice: x: 2, y: 2, z: 4, core: 2. Of those that a mesh axis runs over, the one named last changes fastest.
Arguments:
- tokens: bfloat16 [8192, 1024], P(('dp', 'tensor')), may hold values from -6 to 6
- lengths: int32 [32], replicated, may hold values from 64 to 832, as said below
- seq_order: int32 [32], replicated, may hold values from 0 to 31, as said below
- gain_attn: bfloat16 [1024], P('dp'), may hold values from 0.5 to 1.5
- w_qkv: bfloat16 [3, 1024, 1024], P(None, 'dp', 'tensor'), may hold values from -0.25 to 0.25
- w_attn_out: bfloat16 [1024, 1024], P('tensor', 'dp'), may hold values from -0.375 to 0.375
- gain_mlp: bfloat16 [1024], P('dp'), may hold values from 0.5 to 1.5
- w_in: bfloat16 [1024, 2, 2624], P('dp', None, 'tensor'), may hold values from -0.1875 to 0.1875
- w_mlp_out: bfloat16 [2624, 1024], P('tensor', 'dp'), may hold values from -0.15625 to 0.15625
- cotangent: bfloat16 [8192, 1024], P(('dp', 'tensor')), may hold values from -6 to 6
Outputs:
- output: bfloat16 [8192, 1024], P(('dp', 'tensor'))
- d_tokens: float32 [8192, 1024], P(('dp', 'tensor'))
- d_gain_attn: float32 [1024], P('dp')
- d_w_qkv: float32 [3, 1024, 1024], P(None, 'dp', 'tensor')
- d_w_attn_out: float32 [1024, 1024], P('tensor', 'dp')
- d_gain_mlp: float32 [1024], P('dp')
- d_w_in: float32 [1024, 2, 2624], P('dp', None, 'tensor')
- d_w_mlp_out: float32 [2624, 1024], P('tensor', 'dp')
Inputs may be any that keep to these rules, and one draw needn't show every extreme that they name: For every g the lengths of the sequences seq_order[g * 4] to seq_order[g * 4 + 3] add up to 1024; in every draw some g holds one sequence of the greatest length and 3 of the least. `seq_order`: each sequence number stands once.
All inputs are finite; a program needn't handle non-finite values.
Results may differ from a plain program's by a relative error of at most 0.017.
Values may be sent and summed in bfloat16 or wider, within the bound.
A program may use at most 128 MiB of HBM per device.

v0:
```python
import jax
import jax.numpy as jnp
from jax import lax
from jax.sharding import PartitionSpec as P

HEAD_DIM = 64
SEQ_GRP = 4
rope_base = 160000.0
norm_eps = 1e-05
masked_fill = -1e30


def layer_norm(field_in, norm_gain):
    row_mean = jnp.mean(field_in, axis=-1, keepdims=True)
    centered = field_in - row_mean
    variance = jnp.mean(centered * centered, axis=-1, keepdims=True)
    return centered * lax.rsqrt(variance + norm_eps) * norm_gain


def rotate(field_in, position):
    half_size = field_in.shape[-1] // 2
    index_range = jnp.arange(half_size, dtype=jnp.float32)
    frequency = rope_base ** (-2.0 * index_range / field_in.shape[-1])
    angles = position[:, None] * frequency[None, :]
    cosine = jnp.cos(angles)[:, None, :]
    sine_part = jnp.sin(angles)[:, None, :]
    first_half = field_in[..., :half_size]
    second_half = field_in[..., half_size:]
    return jnp.concatenate(
        [
            first_half * cosine - second_half * sine_part,
            second_half * cosine + first_half * sine_part,
        ],
        axis=-1,
    )


def geglu(act_part, up_part):
    return jax.nn.gelu(act_part, approximate=False) * up_part


def layout(lengths, seq_order, group_rows):
    seq_total = seq_order.shape[0]
    first_seq = lax.axis_index("dp") * SEQ_GRP
    chosen = lax.dynamic_slice_in_dim(seq_order, first_seq, SEQ_GRP)
    matched = chosen[:, None] == jnp.arange(seq_total, dtype=jnp.int32)[None, :]
    dealt_lengths = jnp.sum(jnp.where(matched, lengths[None, :], 0), axis=1)
    seq_ends = jnp.cumsum(dealt_lengths)
    row_index = jnp.arange(group_rows, dtype=jnp.int32)
    passed = row_index[:, None] >= seq_ends[None, :]
    segment = jnp.sum(passed.astype(jnp.int32), axis=1)
    row_start = jnp.sum(jnp.where(passed, dealt_lengths[None, :], 0), axis=1)
    return (segment, (row_index - row_start).astype(jnp.float32))


def item_layout(array_in, block_rows):
    group_rows, head_count, head_size = array_in.shape
    block_count = group_rows // block_rows
    shaped = array_in.reshape(block_count, block_rows, head_count, head_size)
    return shaped.transpose(2, 0, 1, 3).reshape(head_count * block_count, block_rows, head_size)


def from_items(items, group_rows):
    item_count, block_rows, head_size = items.shape
    block_count = group_rows // block_rows
    head_count = item_count // block_count
    shaped = items.reshape(head_count, block_count, block_rows, head_size)
    return shaped.transpose(1, 2, 0, 3).reshape(group_rows, head_count, head_size)


def masked_scores(query_block, key_head, segment_block, segment):
    score_scale = query_block.shape[-1] ** (-0.5)
    raw_scores = lax.dot_general(
        query_block, key_head, (((1,), (1,)), ((), ())), preferred_element_type=jnp.float32
    )
    allowed = segment_block[:, None] == segment[None, :]
    return jnp.where(allowed, raw_scores * score_scale, masked_fill)


def attend_forward(query_rot, key_rot, value_low, segment, block_rows):
    group_rows, head_count, head_size = query_rot.shape
    block_count = group_rows // block_rows
    query_items = item_layout(query_rot, block_rows)
    key_heads = key_rot.transpose(1, 0, 2)
    value_heads = value_low.transpose(1, 0, 2)
    segment_blocks = segment.reshape(block_count, block_rows)

    def one_item(item_index):
        head_index = item_index // block_count
        block_index = item_index % block_count
        query_block = lax.dynamic_index_in_dim(query_items, item_index, 0, False)
        key_head = lax.dynamic_index_in_dim(key_heads, head_index, 0, False)
        value_head = lax.dynamic_index_in_dim(value_heads, head_index, 0, False)
        segment_block = lax.dynamic_index_in_dim(segment_blocks, block_index, 0, False)
        scores = masked_scores(query_block, key_head, segment_block, segment)
        row_top = jnp.max(scores, axis=1, keepdims=True)
        weights = jnp.exp(scores - row_top)
        row_total = jnp.sum(weights, axis=1, keepdims=True)
        probs_low = (weights / row_total).astype(jnp.bfloat16)
        result = jnp.dot(probs_low, value_head, preferred_element_type=jnp.float32)
        return (result, row_top[:, 0] + jnp.log(row_total[:, 0]))

    results, log_totals = lax.map(one_item, jnp.arange(head_count * block_count, dtype=jnp.int32))
    return (from_items(results, group_rows), log_totals)


def attend_backward(query_rot, key_rot, value_low, grad_out, log_totals, segment, block_rows):
    group_rows, head_count, head_size = query_rot.shape
    block_count = group_rows // block_rows
    score_scale = head_size ** (-0.5)
    query_items = item_layout(query_rot, block_rows)
    grad_items = item_layout(grad_out, block_rows)
    key_heads = key_rot.transpose(1, 0, 2)
    value_heads = value_low.transpose(1, 0, 2)
    segment_blocks = segment.reshape(block_count, block_rows)

    def one_item(carried, item_index):
        key_grads, value_grads = carried
        head_index = item_index // block_count
        block_index = item_index % block_count
        query_block = lax.dynamic_index_in_dim(query_items, item_index, 0, False)
        grad_block = lax.dynamic_index_in_dim(grad_items, item_index, 0, False)
        log_row = lax.dynamic_index_in_dim(log_totals, item_index, 0, False)
        key_head = lax.dynamic_index_in_dim(key_heads, head_index, 0, False)
        value_head = lax.dynamic_index_in_dim(value_heads, head_index, 0, False)
        segment_block = lax.dynamic_index_in_dim(segment_blocks, block_index, 0, False)
        scores = masked_scores(query_block, key_head, segment_block, segment)
        prob_full = jnp.exp(scores - log_row[:, None])
        probs_low = prob_full.astype(jnp.bfloat16)
        grad_probs = lax.dot_general(
            grad_block, value_head, (((1,), (1,)), ((), ())), preferred_element_type=jnp.float32
        )
        row_delta = jnp.sum(prob_full * grad_probs, axis=1, keepdims=True)
        grad_scores = (prob_full * (grad_probs - row_delta)).astype(jnp.bfloat16)
        grad_query = (
            jnp.dot(grad_scores, key_head, preferred_element_type=jnp.float32) * score_scale
        )
        grad_key = (
            lax.dot_general(
                grad_scores,
                query_block,
                (((0,), (0,)), ((), ())),
                preferred_element_type=jnp.float32,
            )
            * score_scale
        )
        grad_value = lax.dot_general(
            probs_low, grad_block, (((0,), (0,)), ((), ())), preferred_element_type=jnp.float32
        )
        key_grads = lax.dynamic_update_index_in_dim(
            key_grads,
            lax.dynamic_index_in_dim(key_grads, head_index, 0, False) + grad_key,
            head_index,
            0,
        )
        value_grads = lax.dynamic_update_index_in_dim(
            value_grads,
            lax.dynamic_index_in_dim(value_grads, head_index, 0, False) + grad_value,
            head_index,
            0,
        )
        return ((key_grads, value_grads), grad_query)

    zero_heads = jnp.zeros((head_count, group_rows, head_size), jnp.float32)
    (key_grads, value_grads), query_grads = lax.scan(
        one_item, (zero_heads, zero_heads), jnp.arange(head_count * block_count, dtype=jnp.int32)
    )
    return (
        from_items(query_grads, group_rows),
        key_grads.transpose(1, 0, 2),
        value_grads.transpose(1, 0, 2),
    )


def spread_rows(local_rows):
    return lax.all_gather(local_rows, "tensor", axis=0, tiled=True)


def spread_grads(local_grads):
    return lax.all_gather(local_grads, "tensor", axis=0, tiled=True)


def sum_heads(activations, weight_part, row_count):

    def row_term(first_row, row_number):
        return jnp.dot(activations, weight_part, preferred_element_type=jnp.float32)

    return lax.psum_scatter(
        row_term(jnp.int32(0), row_count * lax.axis_size("tensor")),
        "tensor",
        scatter_dimension=0,
        tiled=True,
    )


def sum_grads(grads_low, weight_full, einsum_form, row_count):

    def row_term(first_row, row_number):
        return jnp.einsum(einsum_form, grads_low, weight_full, preferred_element_type=jnp.float32)

    return lax.psum_scatter(
        row_term(jnp.int32(0), row_count * lax.axis_size("tensor")),
        "tensor",
        scatter_dimension=0,
        tiled=True,
    )


def local(
    tokens, lengths, seq_order, gain_attn, w_qkv, w_attn_out, gain_mlp, w_in, w_mlp_out, cotangent
):
    row_count = tokens.shape[0]
    group_rows = row_count * lax.axis_size("tensor")
    block_rows = min(512, group_rows)
    segment, position = layout(lengths, seq_order, group_rows)
    gain_low_one, qkv_weight, out_weight, gain_low_two, in_weight, down_weight = (
        lax.all_gather(gain_attn, "dp", axis=0, tiled=True),
        lax.all_gather(w_qkv, "dp", axis=1, tiled=True),
        lax.all_gather(w_attn_out, "dp", axis=1, tiled=True),
        lax.all_gather(gain_mlp, "dp", axis=0, tiled=True),
        lax.all_gather(w_in, "dp", axis=0, tiled=True),
        lax.all_gather(w_mlp_out, "dp", axis=1, tiled=True),
    )
    gain_one = gain_low_one.astype(jnp.float32)
    gain_two = gain_low_two.astype(jnp.float32)
    residual = tokens.astype(jnp.float32)
    normed_one = spread_rows(layer_norm(residual, gain_one).astype(jnp.bfloat16))
    qkv = jnp.einsum("rd,pdc->rpc", normed_one, qkv_weight, preferred_element_type=jnp.float32)
    head_count = qkv.shape[2] // HEAD_DIM
    head_shape = (group_rows, head_count, HEAD_DIM)
    query_rot = rotate(qkv[:, 0].reshape(head_shape), position).astype(jnp.bfloat16)
    key_rot = rotate(qkv[:, 1].reshape(head_shape), position).astype(jnp.bfloat16)
    value_low = qkv[:, 2].reshape(head_shape).astype(jnp.bfloat16)
    attended, log_totals = attend_forward(query_rot, key_rot, value_low, segment, block_rows)
    attn_low = attended.reshape(group_rows, head_count * HEAD_DIM).astype(jnp.bfloat16)
    resid_mid = residual + sum_heads(attn_low, out_weight, row_count)
    normed_two = spread_rows(layer_norm(resid_mid, gain_two).astype(jnp.bfloat16))
    gate_up = jnp.einsum("rd,dpc->rpc", normed_two, in_weight, preferred_element_type=jnp.float32)
    hidden = geglu(gate_up[:, 0], gate_up[:, 1]).astype(jnp.bfloat16)
    output = (resid_mid + sum_heads(hidden, down_weight, row_count)).astype(jnp.bfloat16)
    grad_two = spread_grads(cotangent)
    d_hidden = lax.dot_general(
        grad_two, down_weight, (((1,), (1,)), ((), ())), preferred_element_type=jnp.float32
    )
    d_down = lax.dot_general(
        hidden, grad_two, (((0,), (0,)), ((), ())), preferred_element_type=jnp.float32
    )
    geglu_pull = jax.vjp(geglu, gate_up[:, 0], gate_up[:, 1])[1]
    d_act, d_up = geglu_pull(d_hidden)
    d_gate_up = jnp.stack([d_act, d_up], axis=1).astype(jnp.bfloat16)
    d_in = jnp.einsum("rd,rpc->dpc", normed_two, d_gate_up, preferred_element_type=jnp.float32)
    d_normed_two = sum_grads(d_gate_up, in_weight, "rpc,dpc->rd", row_count)
    norm_pull_two = jax.vjp(layer_norm, resid_mid, gain_two)[1]
    d_mid_norm, d_gain_two = norm_pull_two(d_normed_two)
    d_mid = cotangent.astype(jnp.float32) + d_mid_norm
    grad_one = spread_grads(d_mid.astype(jnp.bfloat16))
    d_out = lax.dot_general(
        attn_low, grad_one, (((0,), (0,)), ((), ())), preferred_element_type=jnp.float32
    )
    d_att = lax.dot_general(
        grad_one, out_weight, (((1,), (1,)), ((), ())), preferred_element_type=jnp.float32
    ).astype(jnp.bfloat16)
    d_query_rot, d_key_rot, d_value = attend_backward(
        query_rot, key_rot, value_low, d_att.reshape(head_shape), log_totals, segment, block_rows
    )
    rotate_pull = jax.vjp(lambda field_in: rotate(field_in, position), d_query_rot)[1]
    d_query = rotate_pull(d_query_rot)[0]
    d_key = rotate_pull(d_key_rot)[0]
    flat_shape = (group_rows, head_count * HEAD_DIM)
    d_qkv = jnp.stack(
        [d_query.reshape(flat_shape), d_key.reshape(flat_shape), d_value.reshape(flat_shape)],
        axis=1,
    ).astype(jnp.bfloat16)
    d_qkv_weight = jnp.einsum("rd,rpc->pdc", normed_one, d_qkv, preferred_element_type=jnp.float32)
    d_normed_one = sum_grads(d_qkv, qkv_weight, "rpc,pdc->rd", row_count)
    norm_pull_one = jax.vjp(layer_norm, residual, gain_one)[1]
    d_first, d_gain_one = norm_pull_one(d_normed_one)
    d_tokens = d_mid + d_first
    gain_sums = lax.psum((d_gain_one, d_gain_two), "tensor")
    shares = (
        lax.psum_scatter(gain_sums[0], "dp", scatter_dimension=0, tiled=True),
        lax.psum_scatter(d_qkv_weight, "dp", scatter_dimension=1, tiled=True),
        lax.psum_scatter(d_out, "dp", scatter_dimension=1, tiled=True),
        lax.psum_scatter(gain_sums[1], "dp", scatter_dimension=0, tiled=True),
        lax.psum_scatter(d_in, "dp", scatter_dimension=0, tiled=True),
        lax.psum_scatter(d_down, "dp", scatter_dimension=1, tiled=True),
    )
    return (output, d_tokens, shares[0], shares[1], shares[2], shares[3], shares[4], shares[5])


def solution(mesh):
    return jax.shard_map(
        local,
        mesh=mesh,
        in_specs=(
            P(("dp", "tensor"), None),
            P(),
            P(),
            P("dp"),
            P(None, "dp", "tensor"),
            P("tensor", "dp"),
            P("dp"),
            P("dp", None, "tensor"),
            P("tensor", "dp"),
            P(("dp", "tensor"), None),
        ),
        out_specs=(
            P(("dp", "tensor"), None),
            P(("dp", "tensor"), None),
            P("dp"),
            P(None, "dp", "tensor"),
            P("tensor", "dp"),
            P("dp"),
            P("dp", None, "tensor"),
            P("tensor", "dp"),
        ),
        check_vma=False,
    )
```

profile of v0, /device:TPU:0, one launch (start us, length us, event | category | flops | bytes accessed | tf_op | source)
XLA Modules:
  0.0 1052.6 jit_solution(94516916821931615)
XLA Ops:
  9.1 10.3 all-gather
  24.8 12.0 %all_gather.33 = bf16[256,1024]{1,0:T(8,128)(2,1)} all-gather(bf16[256,128]{1,0:T(8,128)(2,1)S(1)} %copy-done.20), channel_id=1, replica_groups=mesh['dp'=8,'tensor'=4] {'dp'}, dimensions={1}, use_global_device_ids=true | all-gather | bytes 589824 | tf_op jit(solution)/shard_map/all_gather | solution.py:219
  39.8 48.1 %all-gather.10.cloned.1.call-done = bf16[1024,1024]{1,0:T(8,128)(2,1)} async-done(((bf16[256,1024]{1,0:T(8,128)(2,1)}), bf16[1024,1024]{1,0:T(8,128)(2,1)}) %all-gather.10.cloned.1.call-update) | async-done | bytes 2097168 | tf_op jit(solution)/shard_map/all_gather | solution.py:176
  87.9 3.9 fusion.64
  96.9 70.2 %while.32 = (s32[]{:T(128)}, bf16[8,512,64]{1,2,0:T(8,128)(2,1)}, f32[8,512]{1,0:T(8,128)S(1)}, s32[8]{0:T(128)S(1)}, s32[2,512]{1,0:T(2,128)S(1)}, /*index=5*/s...) while((s32[]{:T(128)}, bf16[8,512,64]{1,2,0:T(8,128)(2,1)}, ...), condition=%wide.region_9.10_spmd.clone, body=%wide.region_6.9_spmd.sunk.clone | while | flops 138935840 | bytes 7109525 | solution.py:103
  169.0 3.7 fusion.94
  174.6 8.7 all-gather.1
  183.3 65.1 %reduce-scatter.9.cloned.1.call-done = f32[256,1024]{1,0:T(8,128)} async-done(((f32[1024,1024]{1,0:T(8,128)}), f32[256,1024]{1,0:T(8,128)}) %reduce-scatter.9.cloned.1.call-update) | async-done | bytes 1048592 | tf_op jit(solution)/shard_map/reduce_scatter | solution.py:188
  251.7 24.1 %all-gather.18.cloned.1.call-done = bf16[656,1024]{1,0:T(8,128)(2,1)} async-done(((bf16[656,128]{1,0:T(8,128)(2,1)}), bf16[656,1024]{1,0:T(8,128)(2,1)}) %all-gather.18.cloned.1.call-update) | async-done | bytes 1343504 | tf_op jit(solution)/shard_map/all_gather | solution.py:222
  275.7 47.5 %all-gather.20.cloned.1.call-done = bf16[1024,1024]{1,0:T(8,128)(2,1)} async-done(((bf16[256,1024]{1,0:T(8,128)(2,1)}), bf16[1024,1024]{1,0:T(8,128)(2,1)}) %all-gather.20.cloned.1.call-update) | async-done | bytes 2097168 | tf_op jit(solution)/shard_map/all_gather | solution.py:180
  323.2 5.1 fusion.96
  328.3 26.4 %all-gather.16.cloned.1.call-done = bf16[1024,2,656]{0,2,1:T(8,128)(2,1)} async-done(((bf16[128,2,656]{0,2,1:T(8,128)(2,1)}), bf16[1024,2,656]{0,2,1:T(8,128)(2,1)}) %all-gather.16.cloned.1.call-update) | async-done | bytes 2686992 | tf_op jit(solution)/shard_map/all_gather | solution.py:221
  354.6 48.2 %all-gather.14.cloned.1.call-done = bf16[1024,1024]{1,0:T(8,128)(2,1)} async-done(((bf16[256,1024]{1,0:T(8,128)(2,1)}), bf16[1024,1024]{1,0:T(8,128)(2,1)}) %all-gather.14.cloned.1.call-update) | async-done | bytes 2097168 | tf_op jit(solution)/shard_map/all_gather | solution.py:176
  402.8 5.5 fusion.60
  408.4 6.5 fusion.74
  417.4 5.0 convolution_bitcast_fusion.2
  422.5 5.3 fusion.95
  427.8 70.2 %reduce-scatter.13.cloned.1.call-done = f32[256,1024]{1,0:T(8,128)} async-done(((f32[1024,1024]{1,0:T(8,128)}), f32[256,1024]{1,0:T(8,128)}) %reduce-scatter.13.cloned.1.call-update) | async-done | bytes 1048592 | tf_op jit(solution)/shard_map/reduce_scatter | solution.py:201
  499.6 78.0 %reduce-scatter.11.cloned.1.call-done = f32[256,1024]{1,0:T(8,128)} async-done(((f32[1024,1024]{1,0:T(8,128)}), f32[256,1024]{1,0:T(8,128)}) %reduce-scatter.11.cloned.1.call-update) | async-done | bytes 1048592 | tf_op jit(solution)/shard_map/reduce_scatter | solution.py:188
  582.6 46.4 %all-gather.22.cloned.1.call-done = bf16[1024,1024]{1,0:T(8,128)(2,1)} async-done(((bf16[256,1024]{1,0:T(8,128)(2,1)}), bf16[1024,1024]{1,0:T(8,128)(2,1)}) %all-gather.22.cloned.1.call-update) | async-done | bytes 2097168 | tf_op jit(solution)/shard_map/all_gather | solution.py:180
  635.4 122.5 %while.33 = (s32[]{:T(128)}, f32[4,1024,64]{1,2,0:T(8,128)}, f32[4,1024,64]{1,2,0:T(8,128)}, f32[8,512,64]{1,2,0:T(8,128)}, s32[8]{0:T(128)S(1)}, /*index=5*/s32...) while((s32[]{:T(128)}, f32[4,1024,64]{1,2,0:T(8,128)}, ...), condition=%wide.region_19.20_spmd.clone, body=%wide.region_17.19_spmd.sunk.clone | while | flops 341016096 | bytes 19289032 | solution.py:165
  765.6 5.1 fusion.66
  770.8 5.2 convolution_bitcast_fusion.1
  777.5 4.8 fusion.98
  783.6 7.2 fusion.58
  795.6 20.2 %reduce-scatter.17.cloned.1.call-done = f32[3,128,256]{1,2,0:T(8,128)} async-done(((f32[3,1024,256]{1,2,0:T(8,128)}), f32[3,128,256]{1,2,0:T(8,128)}) %reduce-scatter.17.cloned.1.call-update) | async-done | bytes 393232 | tf_op jit(solution)/shard_map/reduce_scatter | solution.py:282
  817.7 77.0 %reduce-scatter.15.cloned.1.call-done = f32[256,1024]{1,0:T(8,128)} async-done(((f32[1024,1024]{1,0:T(8,128)}), f32[256,1024]{1,0:T(8,128)}) %reduce-scatter.15.cloned.1.call-update) | async-done | bytes 1048592 | tf_op jit(solution)/shard_map/reduce_scatter | solution.py:201
  898.2 14.0 %all-reduce.6 = (f32[1024]{0:T(1024)S(1)}, f32[1024]{0:T(1024)S(1)}) all-reduce(f32[1024]{0:T(1024)S(1)} %get-tuple-element.431, f32[1024]{0:T(1024)S(1)} %get-tuple-element.429), channel_id=6, replica_groups=mesh['dp'=8,'tensor'=4] {'dp'}, use_global_device_ids=true, to_apply=%region_25.26.clone | all-reduce | flops 2048 | bytes 16384
  912.3 11.6 %all-reduce.7 = (f32[128]{0:T(128)}, f32[128]{0:T(128)}) all-reduce(f32[128]{0:T(128)S(1)} %dynamic-slice.1, f32[128]{0:T(128)S(1)} %dynamic-slice.3), channel_id=1, replica_groups=mesh['dp'=8,'tensor'=4] {'tensor'}, use_global_device_ids=true, to_apply=%region_24.25 | all-reduce | flops 256 | bytes 2048 | tf_op jit(solution)/shard_map/psum | solution.py:279
  925.4 19.0 %reduce-scatter.23.cloned.1.call-done = f32[656,128]{1,0:T(8,128)} async-done(((f32[656,1024]{1,0:T(8,128)}), f32[656,128]{1,0:T(8,128)}) %reduce-scatter.23.cloned.1.call-update) | async-done | bytes 335888 | tf_op jit(solution)/shard_map/reduce_scatter | solution.py:286
  944.4 61.5 %reduce-scatter.21.cloned.1.call-done = f32[128,2,656]{0,2,1:T(8,128)} async-done(((f32[1024,2,656]{0,2,1:T(8,128)}), f32[128,2,656]{0,2,1:T(8,128)}) %reduce-scatter.21.cloned.1.call-update) | async-done | bytes 671760 | tf_op jit(solution)/shard_map/reduce_scatter | solution.py:285
  1005.9 40.0 %reduce-scatter.19.cloned.1.call-done = f32[256,128]{1,0:T(8,128)} async-done(((f32[256,1024]{1,0:T(8,128)}), f32[256,128]{1,0:T(8,128)}) %reduce-scatter.19.cloned.1.call-update) | async-done | bytes 131088 | tf_op jit(solution)/shard_map/reduce_scatter | solution.py:283
  (287 shorter events, 188.7 us)
Async XLA Ops:
  7.2 17.0 %copy-start.23 = (s32[32]{0:T(128)S(1)}, s32[32]{0:T(128)}, u32[]{:S(2)}) copy-start(s32[32]{0:T(128)} %param.16) | copy-start | bytes 388
  7.2 17.1 %copy-start.24 = (s32[32]{0:T(128)S(1)}, s32[32]{0:T(128)}, u32[]{:S(2)}) copy-start(s32[32]{0:T(128)} %param.15) | copy-start | bytes 388
  7.2 17.6 %copy-start.20 = (bf16[256,128]{1,0:T(8,128)(2,1)S(1)}, bf16[256,128]{1,0:T(8,128)(2,1)}, u32[]{:S(2)}) copy-start(bf16[256,128]{1,0:T(8,128)(2,1)} %param.19) | copy-start | bytes 196612
  7.2 32.6 %all-gather.12.cloned.1.call-start = ((), (), s32[]{:S(2)}) async-start(), calls=%async_computation.9 | async-start | bytes 1769472 | tf_op jit(solution)/shard_map/all_gather | solution.py:218
  9.0 78.9 %all-gather.10.cloned.1.call-start = ((), (), s32[]{:S(2)}) async-start(), calls=%async_computation.8 | async-start | bytes 2621440 | tf_op jit(solution)/shard_map/all_gather | solution.py:176
  24.1 224.3 %reduce-scatter.9.cloned.1.call-start = ((), (), s32[]{:S(2)}) async-start(), calls=%async_computation.10 | async-start | bytes 5242880 | tf_op jit(solution)/shard_map/reduce_scatter | solution.py:188
  38.2 53.9 %copy-start.16 = (f32[1024,32]{0,1:T(8,128)}, f32[1024,32]{0,1:T(8,128)S(1)}, u32[]{:S(2)}) copy-start(f32[1024,32]{0,1:T(8,128)S(1)} %get-tuple-element.510) | copy-start | bytes 393220
  38.2 53.9 %copy-start.18 = (f32[1024,32]{0,1:T(8,128)}, f32[1024,32]{0,1:T(8,128)S(1)}, u32[]{:S(2)}) copy-start(f32[1024,32]{0,1:T(8,128)S(1)} %get-tuple-element.511) | copy-start | bytes 393220
  172.8 75.7 %copy-start = (bf16[256,1024]{1,0:T(8,128)(2,1)S(1)}, bf16[256,1024]{1,0:T(8,128)(2,1)}, u32[]{:S(2)}) copy-start(bf16[256,1024]{1,0:T(8,128)(2,1)} %param.14) | copy-start | bytes 1572868
  172.8 102.9 %all-gather.18.cloned.1.call-start = ((), (), s32[]{:S(2)}) async-start(), calls=%async_computation.13 | async-start | bytes 1511424 | tf_op jit(solution)/shard_map/all_gather | solution.py:222
  173.4 149.8 %all-gather.20.cloned.1.call-start = ((), (), s32[]{:S(2)}) async-start(), calls=%async_computation.15 | async-start | bytes 2621440 | tf_op jit(solution)/shard_map/all_gather | solution.py:180
  174.0 180.7 %all-gather.16.cloned.1.call-start = ((), (), s32[]{:S(2)}) async-start(), calls=%async_computation.12 | async-start | bytes 3022848 | tf_op jit(solution)/shard_map/all_gather | solution.py:221
  174.6 228.3 %all-gather.14.cloned.1.call-start = ((), (), s32[]{:S(2)}) async-start(), calls=%async_computation.11 | async-start | bytes 2621440 | tf_op jit(solution)/shard_map/all_gather | solution.py:176
  251.2 246.9 %reduce-scatter.13.cloned.1.call-start = ((), (), s32[]{:S(2)}) async-start(), calls=%async_computation.16 | async-start | bytes 5242880 | tf_op jit(solution)/shard_map/reduce_scatter | solution.py:201
  402.8 5.5 copy-start.2
  416.4 6.1 copy-start.14
  422.4 155.2 %reduce-scatter.11.cloned.1.call-start = ((), (), s32[]{:S(2)}) async-start(), calls=%async_computation.14 | async-start | bytes 5242880 | tf_op jit(solution)/shard_map/reduce_scatter | solution.py:188
  427.8 201.2 %all-gather.22.cloned.1.call-start = ((), (), s32[]{:S(2)}) async-start(), calls=%async_computation.17 | async-start | bytes 2621440 | tf_op jit(solution)/shard_map/all_gather | solution.py:180
  499.6 81.7 %copy-start.7 = (bf16[256,1024]{1,0:T(8,128)(2,1)S(1)}, bf16[256,1024]{1,0:T(8,128)(2,1)}, u32[]{:S(2)}) copy-start(bf16[256,1024]{1,0:T(8,128)(2,1)} %param.23) | copy-start | bytes 1572868
  499.6 129.3 %copy-start.10 = (bf16[256,1024]{1,0:T(8,128)(2,1)S(1)}, bf16[256,1024]{1,0:T(8,128)(2,1)}, u32[]{:S(2)}) copy-start(bf16[256,1024]{1,0:T(8,128)(2,1)} %all_gather.33) | copy-start | bytes 1572868
  582.3 233.5 %reduce-scatter.17.cloned.1.call-start = ((), (), s32[]{:S(2)}) async-start(), calls=%async_computation.19 | async-start | bytes 3538944 | tf_op jit(solution)/shard_map/reduce_scatter | solution.py:282
  757.9 5.2 copy-start.1
  757.9 5.2 copy-start.17
  757.9 5.3 copy-start.19
  770.7 124.1 %reduce-scatter.15.cloned.1.call-start = ((), (), s32[]{:S(2)}) async-start(), calls=%async_computation.18 | async-start | bytes 5242880 | tf_op jit(solution)/shard_map/reduce_scatter | solution.py:201
  776.0 168.4 %reduce-scatter.23.cloned.1.call-start = ((), (), s32[]{:S(2)}) async-start(), calls=%async_computation.22 | async-start | bytes 3022848 | tf_op jit(solution)/shard_map/reduce_scatter | solution.py:286
  782.3 223.6 %reduce-scatter.21.cloned.1.call-start = ((), (), s32[]{:S(2)}) async-start(), calls=%async_computation.21 | async-start | bytes 6045696 | tf_op jit(solution)/shard_map/reduce_scatter | solution.py:285
  790.9 3.5 copy-start.25
  790.9 255.0 %reduce-scatter.19.cloned.1.call-start = ((), (), s32[]{:S(2)}) async-start(), calls=%async_computation.20 | async-start | bytes 1179648 | tf_op jit(solution)/shard_map/reduce_scatter | solution.py:283
  794.4 129.6 %copy-start.5 = (f32[256,1024]{1,0:T(8,128)S(1)}, f32[256,1024]{1,0:T(8,128)}, u32[]{:S(2)}) copy-start(f32[256,1024]{1,0:T(8,128)} %copy-done.4) | copy-start | bytes 3145732
  794.4 129.6 %copy-start.8 = (bf16[256,1024]{1,0:T(8,128)(2,1)S(1)}, bf16[256,1024]{1,0:T(8,128)(2,1)}, u32[]{:S(2)}) copy-start(bf16[256,1024]{1,0:T(8,128)(2,1)} %param.23) | copy-start | bytes 1572868
  894.8 29.2 %copy-start.3 = (f32[256,1024]{1,0:T(8,128)S(1)}, f32[256,1024]{1,0:T(8,128)}, u32[]{:S(2)}) copy-start(f32[256,1024]{1,0:T(8,128)} %reduce-scatter.15.cloned.1.call-done) | copy-start | bytes 3145732
  (9 other events, 14.6 us)
Sparse Core Ops, SparseCore 0:
  10.5 29.2 all-gather.11
  42.0 45.9 all-gather.9
  172.9 75.4 reduce-scatter.8
  250.3 25.3 all-gather.17
  277.2 45.9 all-gather.19
  325.1 29.4 all-gather.15
  356.9 45.9 all-gather.13
  422.5 75.4 reduce-scatter.12
  500.3 77.2 reduce-scatter.10
  582.5 46.4 all-gather.21
  770.8 44.9 reduce-scatter.16
  818.0 76.7 reduce-scatter.14
  899.2 45.1 reduce-scatter.22
  948.6 57.1 reduce-scatter.20
  1009.8 36.0 reduce-scatter.18
where the time goes:
time: 1060 us; the launch traced here: 1050 us
  waiting for transfers between devices  675 us (64%)
  matrix products  159 us (15%)
  loops' own time  63.2 us (6%)
  blocking collectives  56.7 us (5%)
  local copies, waits for them, and re-layouts  45.3 us (4%)
  other arithmetic  37.3 us (4%)
  between operations  15.3 us (1%)
    reduce_scatter x2, waiting for transfers between devices, sum_grads(): lax.psum_scatter(row_term(jnp.int32(0), row_count * lax.axis_size('tensor...  147 us
    reduce_scatter x2, waiting for transfers between devices, sum_heads(): lax.psum_scatter(row_term(jnp.int32(0), row_count * lax.axis_size('tensor...  143 us
    all_gather x2, waiting for transfers between devices, spread_rows(): return lax.all_gather(local_rows, 'tensor', axis=0, tiled=True)  96.3 us
    all_gather x2, waiting for transfers between devices, spread_grads(): return lax.all_gather(local_grads, 'tensor', axis=0, tiled=True)  93.8 us
    reduce_scatter x1, waiting for transfers between devices, local(): lax.psum_scatter(d_in, 'dp', scatter_dimension=0, tiled=True)  61.5 us
    reduce_scatter x1, waiting for transfers between devices, local(): lax.psum_scatter(d_out, 'dp', scatter_dimension=1, tiled=True)  40 us
    another operation x1, loops' own time, attend_backward(): lax.scan(one_item, (zero_heads, zero_heads), jnp.arange(head_count * bloc...  31.6 us
    another operation x1, loops' own time, attend_forward(): lax.map(one_item, jnp.arange(head_count * block_count, dtype=jnp.int32))  31.5 us
  transfers between devices with their start and end apart: 15, of which 15 were waited for; matrix products, arithmetic and copies ran while one was open for 5% of the time, Pallas kernels for 0%

commit v1 on v0

--- a/solution.py
+++ b/solution.py
@@ -8,6 +8,28 @@
 rope_base = 160000.0
 norm_eps = 1e-05
 masked_fill = -1e30
+
+
+def drive_stops_all(row_data, chip_axis, array_dim):
+    before, inter, local_next = (
+        lax.axis_size(chip_axis),
+        lax.axis_index(chip_axis),
+        row_data.shape[array_dim],
+    )
+    heap = tuple(((j, (j + 1) % before) for j in range(before)))
+    tall = row_data
+    b = 0
+    big = jnp.zeros(
+        (*row_data.shape[:array_dim], before * local_next, *row_data.shape[array_dim + 1 :]),
+        row_data.dtype,
+    )
+    while b < before:
+        found_now = (inter - b) % before
+        big = lax.dynamic_update_slice_in_dim(big, tall, found_now * local_next, axis=array_dim)
+        if b < before - 1:
+            tall = lax.ppermute(tall, chip_axis, heap)
+        b += 1
+    return big
 
 
 def layer_norm(field_in, norm_gain):
@@ -177,7 +199,7 @@
 
 
 def spread_grads(local_grads):
-    return lax.all_gather(local_grads, "tensor", axis=0, tiled=True)
+    return drive_stops_all(local_grads, "tensor", 0)
 
 
 def sum_heads(activations, weight_part, row_count):

time: 1060 us -> 1020 us (0.962)
  waiting for transfers between devices: 675 us -> 614 us
  local copies, waits for them, and re-layouts: 45.3 us -> 59.2 us
    all_gather x2 -> x0, waiting for transfers between devices: 93.8 us -> none  [spread_grads(): return lax.all_gather(local_grads, 'tensor', axis=0, tiled=True)]
    ppermute x0 -> x6, waiting for transfers between devices: none -> 78 us  [drive_stops_all(): tall = lax.ppermute(tall, chip_axis, heap)]
    all_gather x1, waiting for transfers between devices: 24.1 us -> 0.01 us  [local(): lax.all_gather(w_mlp_out, 'dp', axis=1, tiled=True)]
    all_gather x1, waiting for transfers between devices: 26.4 us -> 5.52 us  [local(): lax.all_gather(w_in, 'dp', axis=0, tiled=True)]
  transfers between devices with their start and end apart: 15 -> 19, of which waited for: 15 -> 18; matrix products, arithmetic and copies ran while one was open for 5% -> 6% of each run, Pallas kernels for 0% -> 0%
where the time goes in v1:
time: 1020 us; the launch traced here: 1010 us
  waiting for transfers between devices  614 us (60%)
  matrix products  158 us (15%)
  loops' own time  63.2 us (6%)
  local copies, waits for them, and re-layouts  59.2 us (6%)
  blocking collectives  56.6 us (6%)
  other arithmetic  36.3 us (4%)
  between operations  15.4 us (2%)
    reduce_scatter x2, waiting for transfers between devices, sum_grads(): lax.psum_scatter(row_term(jnp.int32(0), row_count * lax.axis_size('tensor...  147 us
    reduce_scatter x2, waiting for transfers between devices, sum_heads(): lax.psum_scatter(row_term(jnp.int32(0), row_count * lax.axis_size('tensor...  144 us
    all_gather x2, waiting for transfers between devices, spread_rows(): return lax.all_gather(local_rows, 'tensor', axis=0, tiled=True)  96.1 us
    ppermute x6, waiting for transfers between devices, drive_stops_all(): tall = lax.ppermute(tall, chip_axis, heap)  78 us
    reduce_scatter x1, waiting for transfers between devices, local(): lax.psum_scatter(d_in, 'dp', scatter_dimension=0, tiled=True)  61.5 us
    reduce_scatter x1, waiting for transfers between devices, local(): lax.psum_scatter(d_out, 'dp', scatter_dimension=1, tiled=True)  40.2 us
    another operation x1, loops' own time, attend_backward(): lax.scan(one_item, (zero_heads, zero_heads), jnp.arange(head_count * bloc...  31.6 us
    another operation x1, loops' own time, attend_forward(): lax.map(one_item, jnp.arange(head_count * block_count, dtype=jnp.int32))  31.5 us
  transfers between devices with their start and end apart: 19, of which 18 were waited for; matrix products, arithmetic and copies ran while one was open for 6% of the time, Pallas kernels for 0%

profile of v1, /device:TPU:0, one launch (start us, length us, event | category | flops | bytes accessed | tf_op | source)
XLA Modules:
  0.0 1007.0 jit_solution(9691578149097252202)
XLA Ops:
  9.1 10.3 %all-gather = bf16[8,1,128]{2,1,0:T(2,128)(2,1)S(1)} all-gather(bf16[1,1,128]{2,1,0:T(2,128)(2,1)} %bitcast.332), channel_id=1, replica_groups=mesh['dp'=8,'tensor'=4] {'dp'}, dimensions={0}, use_global_device_ids=true | all-gather | bytes 2304 | tf_op jit(solution)/shard_map/all_gather | solution.py:239
  24.8 12.0 %all_gather.27 = bf16[256,1024]{1,0:T(8,128)(2,1)} all-gather(bf16[256,128]{1,0:T(8,128)(2,1)S(1)} %copy-done.24), channel_id=1, replica_groups=mesh['dp'=8,'tensor'=4] {'dp'}, dimensions={1}, use_global_device_ids=true | all-gather | bytes 589824 | tf_op jit(solution)/shard_map/all_gather | solution.py:241
  39.8 48.1 %all-gather.8.cloned.1.call-done = bf16[1024,1024]{1,0:T(8,128)(2,1)} async-done(((bf16[256,1024]{1,0:T(8,128)(2,1)}), bf16[1024,1024]{1,0:T(8,128)(2,1)}) %all-gather.8.cloned.1.call-update) | async-done | bytes 2097168 | tf_op jit(solution)/shard_map/all_gather | solution.py:198
  96.9 70.2 %while.32 = (s32[]{:T(128)}, bf16[8,512,64]{1,2,0:T(8,128)(2,1)}, f32[8,512]{1,0:T(8,128)S(1)}, s32[8]{0:T(128)S(1)}, s32[2,512]{1,0:T(2,128)S(1)}, /*index=5*/s...) while((s32[]{:T(128)}, bf16[8,512,64]{1,2,0:T(8,128)(2,1)}, ...), condition=%wide.region_9.10_spmd.clone, body=%wide.region_6.9_spmd.sunk.clone | while | flops 138935840 | bytes 7109525 | solution.py:125
  174.0 8.7 all-gather.1
  182.8 65.7 %reduce-scatter.9.cloned.1.call-done = f32[256,1024]{1,0:T(8,128)} async-done(((f32[1024,1024]{1,0:T(8,128)}), f32[256,1024]{1,0:T(8,128)}) %reduce-scatter.9.cloned.1.call-update) | async-done | bytes 1048592 | tf_op jit(solution)/shard_map/reduce_scatter | solution.py:210
  252.8 14.0 %collective-permute-done = bf16[256,1024]{1,0:T(8,128)(2,1)S(1)} collective-permute-done((bf16[256,1024]{1,0:T(8,128)(2,1)S(1)}, bf16[256,1024]{1,0:T(8,128)(2,1)S(1)}, u32[]{:S(2)}, u32[]{:S(2)}) %collective-permute-start) | collective-permute-done | bytes 524320 | tf_op jit(solution)/shard_map/ppermute | solution.py:30
  266.8 14.7 %collective-permute-done.1 = bf16[256,1024]{1,0:T(8,128)(2,1)} collective-permute-done((bf16[256,1024]{1,0:T(8,128)(2,1)S(1)}, bf16[256,1024]{1,0:T(8,128)(2,1)}, u32[]{:S(2)}, u32[]{:S(2)}) %collective-permute-start.1) | collective-permute-done | bytes 524320 | tf_op jit(solution)/shard_map/ppermute | solution.py:30
  287.2 8.8 collective-permute-done.2
  297.8 5.1 fusion.97
  302.9 5.5 all-gather.14.cloned.1.call-done
  308.5 48.0 %all-gather.12.cloned.1.call-done = bf16[1024,1024]{1,0:T(8,128)(2,1)} async-done(((bf16[256,1024]{1,0:T(8,128)(2,1)}), bf16[1024,1024]{1,0:T(8,128)(2,1)}) %all-gather.12.cloned.1.call-update) | async-done | bytes 2097168 | tf_op jit(solution)/shard_map/all_gather | solution.py:198
  356.5 5.5 fusion.60
  362.0 6.5 fusion.74
  371.1 5.0 convolution_bitcast_fusion.2
  376.2 5.3 fusion.96
  381.6 70.2 %reduce-scatter.13.cloned.1.call-done = f32[256,1024]{1,0:T(8,128)} async-done(((f32[1024,1024]{1,0:T(8,128)}), f32[256,1024]{1,0:T(8,128)}) %reduce-scatter.13.cloned.1.call-update) | async-done | bytes 1048592 | tf_op jit(solution)/shard_map/reduce_scatter | solution.py:223
  453.4 77.9 %reduce-scatter.11.cloned.1.call-done = f32[256,1024]{1,0:T(8,128)} async-done(((f32[1024,1024]{1,0:T(8,128)}), f32[256,1024]{1,0:T(8,128)}) %reduce-scatter.11.cloned.1.call-update) | async-done | bytes 1048592 | tf_op jit(solution)/shard_map/reduce_scatter | solution.py:210
  536.5 14.0 %collective-permute-done.3 = bf16[256,1024]{1,0:T(8,128)(2,1)S(1)} collective-permute-done((bf16[256,1024]{1,0:T(8,128)(2,1)S(1)}, bf16[256,1024]{1,0:T(8,128)(2,1)S(1)}, u32[]{:S(2)}, u32[]{:S(2)}) %collective-permute-start.3) | collective-permute-done | bytes 524320 | tf_op jit(solution)/shard_map/ppermute | solution.py:30
  551.3 14.7 %collective-permute-done.4 = bf16[256,1024]{1,0:T(8,128)(2,1)} collective-permute-done((bf16[256,1024]{1,0:T(8,128)(2,1)S(1)}, bf16[256,1024]{1,0:T(8,128)(2,1)}, u32[]{:S(2)}, u32[]{:S(2)}) %collective-permute-start.4) | collective-permute-done | bytes 524320 | tf_op jit(solution)/shard_map/ppermute | solution.py:30
  568.5 11.8 %collective-permute-done.5 = bf16[256,1024]{1,0:T(8,128)(2,1)} collective-permute-done((bf16[256,1024]{1,0:T(8,128)(2,1)}, bf16[256,1024]{1,0:T(8,128)(2,1)}, u32[]{:S(2)}, u32[]{:S(2)}) %collective-permute-start.5) | collective-permute-done | bytes 524320 | tf_op jit(solution)/shard_map/ppermute | solution.py:30
  589.9 122.8 %while.33 = (s32[]{:T(128)}, f32[4,1024,64]{1,2,0:T(8,128)}, f32[4,1024,64]{1,2,0:T(8,128)}, f32[8,512,64]{1,2,0:T(8,128)}, s32[8]{0:T(128)S(1)}, /*index=5*/s32...) while((s32[]{:T(128)}, f32[4,1024,64]{1,2,0:T(8,128)}, ...), condition=%wide.region_19.20_spmd.clone, body=%wide.region_17.19_spmd.sunk.clone | while | flops 341016096 | bytes 19289032 | solution.py:187
  720.4 5.1 fusion.66
  725.5 5.2 convolution_bitcast_fusion.1
  738.4 7.3 fusion.58
  750.2 19.8 %reduce-scatter.17.cloned.1.call-done = f32[3,128,256]{1,2,0:T(8,128)} async-done(((f32[3,1024,256]{1,2,0:T(8,128)}), f32[3,128,256]{1,2,0:T(8,128)}) %reduce-scatter.17.cloned.1.call-update) | async-done | bytes 393232 | tf_op jit(solution)/shard_map/reduce_scatter | solution.py:304
  771.9 77.0 %reduce-scatter.15.cloned.1.call-done = f32[256,1024]{1,0:T(8,128)} async-done(((f32[1024,1024]{1,0:T(8,128)}), f32[256,1024]{1,0:T(8,128)}) %reduce-scatter.15.cloned.1.call-update) | async-done | bytes 1048592 | tf_op jit(solution)/shard_map/reduce_scatter | solution.py:223
  852.4 13.9 %all-reduce.6 = (f32[1024]{0:T(1024)S(1)}, f32[1024]{0:T(1024)S(1)}) all-reduce(f32[1024]{0:T(1024)S(1)} %get-tuple-element.431, f32[1024]{0:T(1024)S(1)} %get-tuple-element.429), channel_id=6, replica_groups=mesh['dp'=8,'tensor'=4] {'dp'}, use_global_device_ids=true, to_apply=%region_25.26.clone | all-reduce | flops 2048 | bytes 16384
  866.5 11.7 %all-reduce.7 = (f32[128]{0:T(128)}, f32[128]{0:T(128)}) all-reduce(f32[128]{0:T(128)S(1)} %dynamic-slice.1, f32[128]{0:T(128)S(1)} %dynamic-slice.3), channel_id=1, replica_groups=mesh['dp'=8,'tensor'=4] {'tensor'}, use_global_device_ids=true, to_apply=%region_24.25 | all-reduce | flops 256 | bytes 2048 | tf_op jit(solution)/shard_map/psum | solution.py:301
  879.6 19.0 %reduce-scatter.23.cloned.1.call-done = f32[656,128]{1,0:T(8,128)} async-done(((f32[656,1024]{1,0:T(8,128)}), f32[656,128]{1,0:T(8,128)}) %reduce-scatter.23.cloned.1.call-update) | async-done | bytes 335888 | tf_op jit(solution)/shard_map/reduce_scatter | solution.py:308
  898.6 61.5 %reduce-scatter.21.cloned.1.call-done = f32[128,2,656]{0,2,1:T(8,128)} async-done(((f32[1024,2,656]{0,2,1:T(8,128)}), f32[128,2,656]{0,2,1:T(8,128)}) %reduce-scatter.21.cloned.1.call-update) | async-done | bytes 671760 | tf_op jit(solution)/shard_map/reduce_scatter | solution.py:307
  960.1 40.2 %reduce-scatter.19.cloned.1.call-done = f32[256,128]{1,0:T(8,128)} async-done(((f32[256,1024]{1,0:T(8,128)}), f32[256,128]{1,0:T(8,128)}) %reduce-scatter.19.cloned.1.call-update) | async-done | bytes 131088 | tf_op jit(solution)/shard_map/reduce_scatter | solution.py:305
  (310 shorter events, 215.9 us)
Async XLA Ops:
  7.2 17.0 %copy-start.27 = (s32[32]{0:T(128)S(1)}, s32[32]{0:T(128)}, u32[]{:S(2)}) copy-start(s32[32]{0:T(128)} %param.16) | copy-start | bytes 388
  7.2 17.1 %copy-start.28 = (s32[32]{0:T(128)S(1)}, s32[32]{0:T(128)}, u32[]{:S(2)}) copy-start(s32[32]{0:T(128)} %param.15) | copy-start | bytes 388
  7.2 17.6 %copy-start.24 = (bf16[256,128]{1,0:T(8,128)(2,1)S(1)}, bf16[256,128]{1,0:T(8,128)(2,1)}, u32[]{:S(2)}) copy-start(bf16[256,128]{1,0:T(8,128)(2,1)} %param.19) | copy-start | bytes 196612
  7.2 32.6 %all-gather.10.cloned.1.call-start = ((), (), s32[]{:S(2)}) async-start(), calls=%async_computation.9 | async-start | bytes 1769472 | tf_op jit(solution)/shard_map/all_gather | solution.py:240
  9.0 78.9 %all-gather.8.cloned.1.call-start = ((), (), s32[]{:S(2)}) async-start(), calls=%async_computation.8 | async-start | bytes 2621440 | tf_op jit(solution)/shard_map/all_gather | solution.py:198
  24.1 224.3 %reduce-scatter.9.cloned.1.call-start = ((), (), s32[]{:S(2)}) async-start(), calls=%async_computation.10 | async-start | bytes 5242880 | tf_op jit(solution)/shard_map/reduce_scatter | solution.py:210
  38.2 53.9 %copy-start.19 = (f32[1024,32]{0,1:T(8,128)}, f32[1024,32]{0,1:T(8,128)S(1)}, u32[]{:S(2)}) copy-start(f32[1024,32]{0,1:T(8,128)S(1)} %get-tuple-element.512) | copy-start | bytes 393220
  38.2 53.9 %copy-start.21 = (f32[1024,32]{0,1:T(8,128)}, f32[1024,32]{0,1:T(8,128)S(1)}, u32[]{:S(2)}) copy-start(f32[1024,32]{0,1:T(8,128)S(1)} %get-tuple-element.513) | copy-start | bytes 393220
  172.8 75.7 %copy-start = (bf16[256,1024]{1,0:T(8,128)(2,1)S(1)}, bf16[256,1024]{1,0:T(8,128)(2,1)}, u32[]{:S(2)}) copy-start(bf16[256,1024]{1,0:T(8,128)(2,1)} %param.14) | copy-start | bytes 1572868
  172.8 125.0 %all-gather.16.cloned.1.call-start = ((), (), s32[]{:S(2)}) async-start(), calls=%async_computation.13 | async-start | bytes 1511424 | tf_op jit(solution)/shard_map/all_gather | solution.py:244
  173.4 135.1 %all-gather.14.cloned.1.call-start = ((), (), s32[]{:S(2)}) async-start(), calls=%async_computation.12 | async-start | bytes 3022848 | tf_op jit(solution)/shard_map/all_gather | solution.py:243
  174.0 182.5 %all-gather.12.cloned.1.call-start = ((), (), s32[]{:S(2)}) async-start(), calls=%async_computation.11 | async-start | bytes 2621440 | tf_op jit(solution)/shard_map/all_gather | solution.py:198
  182.8 68.5 %copy-start.9 = (bf16[256,1024]{1,0:T(8,128)(2,1)S(1)}, bf16[256,1024]{1,0:T(8,128)(2,1)}, u32[]{:S(2)}) copy-start(bf16[256,1024]{1,0:T(8,128)(2,1)} %param.23) | copy-start | bytes 1572868
  251.2 200.6 %reduce-scatter.13.cloned.1.call-start = ((), (), s32[]{:S(2)}) async-start(), calls=%async_computation.15 | async-start | bytes 5242880 | tf_op jit(solution)/shard_map/reduce_scatter | solution.py:223
  251.2 15.5 %collective-permute-start = (bf16[256,1024]{1,0:T(8,128)(2,1)S(1)}, bf16[256,1024]{1,0:T(8,128)(2,1)S(1)}, u32[]{:S(2)}, u32[]{:S(2)}) collective-permute-start(bf16[256,1024]{1,0:T(8,128)(2,1)S(1)} %copy-done.9), channel_id=1, source_target_pairs={{0,1},{1,2},{2,3},{3,0},{4,5},{5,6},{6,7},{7,4},{8,9},{9,10},{10,1... | collective-permute-start | bytes 1572872 | tf_op jit(solution)/shard_map/ppermute | solution.py:30
  266.8 14.7 %collective-permute-start.1 = (bf16[256,1024]{1,0:T(8,128)(2,1)S(1)}, bf16[256,1024]{1,0:T(8,128)(2,1)}, u32[]{:S(2)}, u32[]{:S(2)}) collective-permute-start(bf16[256,1024]{1,0:T(8,128)(2,1)S(1)} %collective-permute-done), channel_id=1, source_target_pairs={{0,1},{1,2},{2,3},{3,0},{4,5},{5,6},{6,7},{7,4},{8,9},{9,10},{10,1... | collective-permute-start | bytes 1572872 | tf_op jit(solution)/shard_map/ppermute | solution.py:30
  281.5 14.5 %collective-permute-start.2 = (bf16[256,1024]{1,0:T(8,128)(2,1)}, bf16[256,1024]{1,0:T(8,128)(2,1)}, u32[]{:S(2)}, u32[]{:S(2)}) collective-permute-start(bf16[256,1024]{1,0:T(8,128)(2,1)} %collective-permute-done.1), channel_id=1, source_target_pairs={{0,1},{1,2},{2,3},{3,0},{4,5},{5,6},{6,7},{7,4},{8,9},{9,10},{10,1... | collective-permute-start | bytes 1572872 | tf_op jit(solution)/shard_map/ppermute | solution.py:30
  370.0 6.1 copy-start.17
  376.1 155.2 %reduce-scatter.11.cloned.1.call-start = ((), (), s32[]{:S(2)}) async-start(), calls=%async_computation.14 | async-start | bytes 5242880 | tf_op jit(solution)/shard_map/reduce_scatter | solution.py:210
  381.5 388.5 %reduce-scatter.17.cloned.1.call-start = ((), (), s32[]{:S(2)}) async-start(), calls=%async_computation.17 | async-start | bytes 3538944 | tf_op jit(solution)/shard_map/reduce_scatter | solution.py:304
  451.7 79.6 %copy-start.12 = (f32[256,1024]{1,0:T(8,128)S(1)}, f32[256,1024]{1,0:T(8,128)}, u32[]{:S(2)}) copy-start(f32[256,1024]{1,0:T(8,128)} %reduce-scatter.13.cloned.1.call-done) | copy-start | bytes 3145732
  535.0 15.5 %collective-permute-start.3 = (bf16[256,1024]{1,0:T(8,128)(2,1)S(1)}, bf16[256,1024]{1,0:T(8,128)(2,1)S(1)}, u32[]{:S(2)}, u32[]{:S(2)}) collective-permute-start(bf16[256,1024]{1,0:T(8,128)(2,1)S(1)} %get-tuple-element.482), channel_id=1, source_target_pairs={{0,1},{1,2},{2,3},{3,0},{4,5},{5,6},{6,7},{7,4},{8,9},{9,10},{10,1... | collective-permute-start | bytes 1572872 | tf_op jit(solution)/shard_map/ppermute | solution.py:30
  551.3 14.7 %collective-permute-start.4 = (bf16[256,1024]{1,0:T(8,128)(2,1)S(1)}, bf16[256,1024]{1,0:T(8,128)(2,1)}, u32[]{:S(2)}, u32[]{:S(2)}) collective-permute-start(bf16[256,1024]{1,0:T(8,128)(2,1)S(1)} %collective-permute-done.3), channel_id=1, source_target_pairs={{0,1},{1,2},{2,3},{3,0},{4,5},{5,6},{6,7},{7,4},{8,9},{9,10},{10,1... | collective-permute-start | bytes 1572872 | tf_op jit(solution)/shard_map/ppermute | solution.py:30
  566.1 14.2 %collective-permute-start.5 = (bf16[256,1024]{1,0:T(8,128)(2,1)}, bf16[256,1024]{1,0:T(8,128)(2,1)}, u32[]{:S(2)}, u32[]{:S(2)}) collective-permute-start(bf16[256,1024]{1,0:T(8,128)(2,1)} %collective-permute-done.4), channel_id=1, source_target_pairs={{0,1},{1,2},{2,3},{3,0},{4,5},{5,6},{6,7},{7,4},{8,9},{9,10},{10,1... | collective-permute-start | bytes 1572872 | tf_op jit(solution)/shard_map/ppermute | solution.py:30
  566.2 15.1 %copy-start.13 = (bf16[256,1024]{1,0:T(8,128)(2,1)S(1)}, bf16[256,1024]{1,0:T(8,128)(2,1)}, u32[]{:S(2)}) copy-start(bf16[256,1024]{1,0:T(8,128)(2,1)} %all_gather.27) | copy-start | bytes 1572868
  725.5 123.5 %reduce-scatter.15.cloned.1.call-start = ((), (), s32[]{:S(2)}) async-start(), calls=%async_computation.16 | async-start | bytes 5242880 | tf_op jit(solution)/shard_map/reduce_scatter | solution.py:223
  730.8 167.8 %reduce-scatter.23.cloned.1.call-start = ((), (), s32[]{:S(2)}) async-start(), calls=%async_computation.20 | async-start | bytes 3022848 | tf_op jit(solution)/shard_map/reduce_scatter | solution.py:308
  737.0 223.0 %reduce-scatter.21.cloned.1.call-start = ((), (), s32[]{:S(2)}) async-start(), calls=%async_computation.19 | async-start | bytes 6045696 | tf_op jit(solution)/shard_map/reduce_scatter | solution.py:307
  745.7 254.6 %reduce-scatter.19.cloned.1.call-start = ((), (), s32[]{:S(2)}) async-start(), calls=%async_computation.18 | async-start | bytes 1179648 | tf_op jit(solution)/shard_map/reduce_scatter | solution.py:305
  748.9 129.2 %copy-start.5 = (f32[256,1024]{1,0:T(8,128)S(1)}, f32[256,1024]{1,0:T(8,128)}, u32[]{:S(2)}) copy-start(f32[256,1024]{1,0:T(8,128)} %copy-done.4) | copy-start | bytes 3145732
  748.9 129.2 %copy-start.11 = (bf16[256,1024]{1,0:T(8,128)(2,1)S(1)}, bf16[256,1024]{1,0:T(8,128)(2,1)}, u32[]{:S(2)}) copy-start(bf16[256,1024]{1,0:T(8,128)(2,1)} %param.23) | copy-start | bytes 1572868
  849.0 29.2 %copy-start.3 = (f32[256,1024]{1,0:T(8,128)S(1)}, f32[256,1024]{1,0:T(8,128)}, u32[]{:S(2)}) copy-start(f32[256,1024]{1,0:T(8,128)} %reduce-scatter.15.cloned.1.call-done) | copy-start | bytes 3145732
  (17 other events, 44.2 us)
Sparse Core Ops, SparseCore 0:
  10.5 29.2 all-gather.9
  42.0 45.9 all-gather.7
  172.9 75.4 reduce-scatter.8
  250.3 25.3 all-gather.15
  277.6 30.7 all-gather.13
  310.5 45.9 all-gather.11
  376.2 75.4 reduce-scatter.12
  454.0 77.2 reduce-scatter.10
  725.6 44.3 reduce-scatter.16
  772.2 76.7 reduce-scatter.14
  853.4 45.1 reduce-scatter.22
  902.8 57.1 reduce-scatter.20
  964.1 36.0 reduce-scatter.18
